TPU v7x, 256 devices: a whole 4x4x8 slice. The times are simulated.
256 devices in a mesh: enc: 16 (over z, core), vocab: 8 (over x, y_hi), grp: 2 (over y_lo).
Axes of the slice: x: 4, y: 4 (y_hi: 2, y_lo: 2; y = y_hi * 2 + y_lo), z: 8, core: 2. Of those that a mesh axis runs over, the one named last changes fastest.
Arguments:
- hidden: bfloat16 [12288, 1024], P('enc', ('vocab', 'grp')), may hold values from -6 to 6
- dense_weight: bfloat16 [1024, 1024], P('enc'), may hold values from -0.1875 to 0.1875
- head_weight: bfloat16 [1024, 126976], P('enc', ('vocab', 'grp')), may hold values from -0.1875 to 0.1875
- head_bias: float32 [126976], P(('vocab', 'grp')), may hold values from -4 to 4
- lengths: int32 [48], P('enc'), may hold values from 64 to 256, as said below
- queries: bfloat16 [128, 126976], P('enc', ('vocab', 'grp')), may hold values from -0.25 to 0.25283518
- positives: int32 [128], replicated, may hold values from 0 to 47
Outputs:
- batch_loss: float32 [], replicated
- query_grad: float32 [128, 126976], P('enc', ('vocab', 'grp'))
- passage_grad: float32 [48, 126976], P('enc', ('vocab', 'grp'))
Inputs may be any that keep to these rules, and one draw needn't show every extreme that they name: `lengths`: each 3 passages in a row hold, among their first two, one with 256 valid tokens and one with 64.
All inputs are finite; a program needn't handle non-finite values.
Results may differ from a plain program's by a relative error of at most 0.035.
Values may be sent and summed in bfloat16 or wider, within the bound.
A program may use at most 128 MiB of HBM per device.

v0:
```python
import jax
import jax.numpy as jnp
from jax import lax
from jax.sharding import PartitionSpec as P


def finish_norm(pre_act):
    activated = jax.nn.gelu(pre_act, approximate=False)
    center = jnp.mean(activated, axis=-1, keepdims=True)
    spread = jnp.mean(jnp.square(activated - center), axis=-1, keepdims=True)
    return ((activated - center) * lax.rsqrt(spread + 1e-05)).astype(jnp.bfloat16)


def project(in_rows, dense_weight):
    pre_act = jnp.dot(
        in_rows,
        lax.all_gather(dense_weight, "enc", axis=0, tiled=True),
        preferred_element_type=jnp.float32,
    )
    return finish_norm(pre_act)


def pool_reps(logits, token_counts, seq_len):
    passages = token_counts.shape[0]
    by_passage = logits.reshape(passages, seq_len, logits.shape[1])
    positions = lax.broadcasted_iota(jnp.int32, (passages, seq_len), 1)
    is_valid = positions < token_counts[:, None]
    masked = jnp.where(is_valid[:, :, None], by_passage, -jnp.inf)
    peak_val = jnp.max(masked, axis=1)
    return jnp.log1p(jnp.maximum(peak_val, 0.0)).astype(jnp.bfloat16)


def softmax_grads(scores, chosen):
    peak_val = jnp.max(scores, axis=1, keepdims=True)
    log_total = jnp.log(jnp.sum(jnp.exp(scores - peak_val), axis=1, keepdims=True)) + peak_val
    columns = lax.broadcasted_iota(jnp.int32, scores.shape, 1)
    is_positive = columns == chosen[:, None]
    picked_score = jnp.sum(jnp.where(is_positive, scores, 0.0), axis=1)
    batch_loss = jnp.sum(log_total[:, 0] - picked_score)
    score_grad = (jnp.exp(scores - log_total) - is_positive.astype(jnp.float32)).astype(
        jnp.bfloat16
    )
    return (batch_loss, score_grad)


def per_device(hidden, dense_weight, head_weight, head_bias, lengths, queries, positives):
    pass_dev = lengths.shape[0]
    seq_len = hidden.shape[0] // pass_dev
    enc_index = lax.axis_index("enc")
    features_all = lax.all_gather(hidden, ("vocab", "grp"), axis=1, tiled=True)
    normed = project(features_all, dense_weight)
    logits = jnp.dot(
        normed,
        lax.all_gather(head_weight, "enc", axis=0, tiled=True),
        preferred_element_type=jnp.float32,
    )
    pass_reps = pool_reps(logits + head_bias, lengths, seq_len)
    all_queries = lax.all_gather(queries, "enc", axis=0, tiled=True)
    partial_value = lax.dot_general(
        all_queries, pass_reps, (((1,), (1,)), ((), ())), preferred_element_type=jnp.float32
    )
    local_scores = lax.psum(partial_value, ("vocab", "grp"))
    scores = lax.all_gather(local_scores, "enc", axis=1, tiled=True)
    loss_sum, score_grad = softmax_grads(scores, positives)
    batch_loss = loss_sum / scores.shape[0]
    own_grad = lax.dynamic_slice_in_dim(score_grad, enc_index * pass_dev, pass_dev, 1)
    query_grad = lax.psum_scatter(
        jnp.dot(own_grad, pass_reps, preferred_element_type=jnp.float32),
        "enc",
        scatter_dimension=0,
        tiled=True,
    )
    passage_grad = lax.dot_general(
        own_grad, all_queries, (((0,), (0,)), ((), ())), preferred_element_type=jnp.float32
    )
    return (batch_loss, query_grad, passage_grad)


def solution(mesh):
    placed = (
        P("enc", ("vocab", "grp")),
        P("enc", None),
        P("enc", ("vocab", "grp")),
        P(("vocab", "grp")),
        P("enc"),
        P("enc", ("vocab", "grp")),
        P(),
    )
    return jax.shard_map(
        per_device,
        mesh=mesh,
        in_specs=placed,
        out_specs=(P(), P("enc", ("vocab", "grp")), P("enc", ("vocab", "grp"))),
        check_vma=False,
    )
```

profile of v0, /device:TPU:2, one launch (start us, length us, event | category | flops | bytes accessed | tf_op | source)
XLA Modules:
  0.0 363.2 jit_solution(3995243074012879067)
XLA Ops:
  7.2 0.0 all-gather.6.cloned.1.call-start
  7.2 0.7 all-gather.6.cloned.1.call-update
  7.9 0.0 all-gather.8.cloned.1.call-start
  7.9 0.7 all-gather.8.cloned.1.call-update
  8.6 0.0 all-gather.10.cloned.1.call-start
  8.7 0.7 all-gather.10.cloned.1.call-update
  9.4 0.0 all-gather.12.cloned.1.call-start
  9.4 0.5 all-gather.12.cloned.1.call-update
  10.0 0.0 reduce-scatter.2.cloned.1.call-start
  10.0 0.7 iota_compare_fusion.1
  10.7 0.7 iota_compare_fusion
  11.4 50.6 %all-gather.6.cloned.1.call-done = bf16[768,1024]{0,1:T(8,128)(2,1)} async-done(((bf16[768,64]{0,1:T(8,128)(2,1)}), bf16[768,1024]{0,1:T(8,128)(2,1)}) %all-gather.6.cloned.1.call-update) | async-done | bytes 1572880 | tf_op jit(solution)/shard_map/all_gather | solution.py:50
  62.0 41.4 %all-gather.8.cloned.1.call-done = bf16[1024,1024]{1,0:T(8,128)(2,1)} async-done(((bf16[64,1024]{1,0:T(8,128)(2,1)}), bf16[1024,1024]{1,0:T(8,128)(2,1)}) %all-gather.8.cloned.1.call-update) | async-done | bytes 2097168 | tf_op jit(solution)/shard_map/all_gather | solution.py:17
  103.4 10.5 %fusion.17 = (f32[768]{0:T(1024)S(1)}, f32[768,1024]{1,0:T(8,128)S(1)}) fusion(bf16[768,1024]{0,1:T(8,128)(2,1)} %all-gather.6.cloned.1.call-done, bf16[1024,1024]{1,0:T(8,128)(2,1)} %all-gather.8.cloned.1.call-done), kind=kOutput, calls=%fused_computation.41 | convolution fusion | flops 1661730048 | bytes 6818816 | tf_op jit(solution)/shard_map/dot_general | solution.py:15
  114.0 0.0 copy-start.2
  114.0 0.4 multiply_reduce_fusion
  114.5 82.1 %all-gather.10.cloned.1.call-done = bf16[1024,7936]{1,0:T(8,128)(2,1)} async-done(((bf16[64,7936]{1,0:T(8,128)(2,1)}), bf16[1024,7936]{1,0:T(8,128)(2,1)}) %all-gather.10.cloned.1.call-update) | async-done | bytes 16252944 | tf_op jit(solution)/shard_map/all_gather | solution.py:54
  196.5 0.0 copy-done.2
  196.5 21.4 %convolution_add_fusion = f32[768,7936]{1,0:T(8,128)} fusion(bf16[1024,7936]{1,0:T(8,128)(2,1)} %all-gather.10.cloned.1.call-done, f32[7936]{0:T(1024)S(1)} %copy-done.2, f32[768,1024]{1,0:T(8,128)S(1)} %get-tuple-element.8, f32[768]{0:T(1024)S(1)} %add_rsqrt_fusion, f32[768]{0:T(1024)S(1)} %broadcast_multiply_fusion), kind=kOutput, calls=%fused_computation.1 | convolution fusion | flops 12490702848 | bytes 43815936 | tf_op jit(solution)/shard_map/dot_general | solution.py:52
  217.9 0.0 copy-start.1
  217.9 9.4 %select_reduce_fusion = f32[3,7936]{1,0:T(4,128)S(1)} fusion(f32[3,256,7936]{2,1,0:T(8,128)} %bitcast.14, pred[3,256]{1,0:T(4,128)(4,1)S(1)} %iota_compare_fusion.1), kind=kLoop, calls=%fused_computation | loop fusion | flops 12165888 | bytes 24475392 | tf_op jit(solution)/shard_map/reduce_max | solution.py:29
  227.4 9.2 %all-gather.12.cloned.1.call-done = bf16[128,7936]{1,0:T(8,128)(2,1)} async-done(((bf16[8,7936]{1,0:T(8,128)(2,1)}), bf16[128,7936]{1,0:T(8,128)(2,1)}) %all-gather.12.cloned.1.call-update) | async-done | bytes 2031632 | tf_op jit(solution)/shard_map/all_gather | solution.py:58
  236.5 2.2 convolution_bitcast_fusion
  238.7 34.3 %psum.7 = f32[128,3]{0,1:T(4,128)S(1)} all-reduce(f32[128,3]{0,1:T(4,128)S(1)} %convolution_bitcast_fusion), channel_id=1, replica_groups=mesh['enc'=16,'vocab'=8,'grp'=2] {'vocab','grp'}, use_global_device_ids=true, to_apply=%region_3.4 | all-reduce | flops 384 | bytes 3072 | tf_op jit(solution)/shard_map/psum | solution.py:62
  273.0 15.7 %all-gather = f32[16,3,128]{2,1,0:T(4,128)S(1)} all-gather(f32[1,3,128]{2,1,0:T(4,128)S(1)} %bitcast.17), channel_id=1, replica_groups=mesh['enc'=16,'vocab'=8,'grp'=2] {'enc'}, dimensions={0}, use_global_device_ids=true | all-gather | bytes 26112 | tf_op jit(solution)/shard_map/all_gather | solution.py:63
  288.7 0.0 copy-done.1
  288.8 0.6 subtract_reduce_fusion
  289.4 2.7 fusion.14
  292.0 0.0 reduce-scatter.2.cloned.1.call-update
  292.7 0.0 copy-done
  292.7 1.0 fusion.20
  293.8 61.7 %reduce-scatter.2.cloned.1.call-done = f32[8,7936]{1,0:T(8,128)} async-done(((f32[128,7936]{1,0:T(8,128)}), f32[8,7936]{1,0:T(8,128)}) %reduce-scatter.2.cloned.1.call-update) | async-done | bytes 253968 | tf_op jit(solution)/shard_map/reduce_scatter | solution.py:67
  (6 shorter events, 0.1 us)
Async XLA Ops:
  7.2 54.9 %all-gather.6.cloned.1.call-start = ((), (), s32[]{:S(2)}) async-start(), calls=%async_computation.1 | async-start | bytes 1671168 | tf_op jit(solution)/shard_map/all_gather | solution.py:50
  7.9 95.5 %all-gather.8.cloned.1.call-start = ((), (), s32[]{:S(2)}) async-start(), calls=%async_computation.2 | async-start | bytes 2228224 | tf_op jit(solution)/shard_map/all_gather | solution.py:17
  8.6 187.9 %all-gather.10.cloned.1.call-start = ((), (), s32[]{:S(2)}) async-start(), calls=%async_computation.3 | async-start | bytes 17268736 | tf_op jit(solution)/shard_map/all_gather | solution.py:54
  9.4 227.2 %all-gather.12.cloned.1.call-start = ((), (), s32[]{:S(2)}) async-start(), calls=%async_computation.4 | async-start | bytes 2158592 | tf_op jit(solution)/shard_map/all_gather | solution.py:58
  10.0 345.5 %reduce-scatter.2.cloned.1.call-start = ((), (), s32[]{:S(2)}) async-start(), calls=%async_computation.5 | async-start | bytes 4317184 | tf_op jit(solution)/shard_map/reduce_scatter | solution.py:67
  114.0 82.6 %copy-start.2 = (f32[7936]{0:T(1024)S(1)}, f32[7936]{0:T(1024)}, u32[]{:S(2)}) copy-start(f32[7936]{0:T(1024)} %param.10) | copy-start | bytes 95236
  217.9 70.8 %copy-start.1 = (s32[128]{0:T(128)S(1)}, s32[128]{0:T(128)}, u32[]{:S(2)}) copy-start(s32[128]{0:T(128)} %param.13) | copy-start | bytes 1540
  289.4 3.3 copy-start
Sparse Core Ops, SparseCore 0:
  10.5 51.5 all-gather.5
  63.9 39.5 all-gather.7
  105.3 91.2 all-gather.9
  198.2 38.2 all-gather.11
  292.2 63.2 reduce-scatter.1
where the time goes:
time: 363 us
  waiting for transfers between devices  248 us (68%)
  blocking collectives  50 us (14%)
  matrix products  37.8 us (10%)
  between operations  15.6 us (4%)
  other arithmetic  12 us (3%)
    all_gather x1, waiting for transfers between devices, per_device(): lax.all_gather(head_weight, 'enc', axis=0, tiled=True)  82.1 us
    reduce_scatter x1, waiting for transfers between devices, per_device(): lax.psum_scatter(jnp.dot(own_grad, pass_reps, preferred_element_type=jnp....  61.7 us
    all_gather x1, waiting for transfers between devices, per_device(): features_all = lax.all_gather(hidden, ('vocab', 'grp'), axis=1, tiled=True)  50.6 us
    all_gather x1, waiting for transfers between devices, project(): lax.all_gather(dense_weight, 'enc', axis=0, tiled=True)  41.4 us
    psum x1, blocking collectives, per_device(): local_scores = lax.psum(partial_value, ('vocab', 'grp'))  34.3 us
    dot_general x1, matrix products, per_device(): jnp.dot(normed, lax.all_gather(head_weight, 'enc', axis=0, tiled=True), p...  21.4 us
    all_gather x1, blocking collectives, per_device(): scores = lax.all_gather(local_scores, 'enc', axis=1, tiled=True)  15.7 us
    dot_general x1, matrix products, project(): jnp.dot(in_rows, lax.all_gather(dense_weight, 'enc', axis=0, tiled=True),...  10.5 us
  transfers between devices with their start and end apart: 5, of which 5 were waited for; matrix products, arithmetic and copies ran while one was open for 12% of the time, Pallas kernels for 0%

commit v1 on v0

--- a/solution.py
+++ b/solution.py
@@ -59,7 +59,7 @@
     partial_value = lax.dot_general(
         all_queries, pass_reps, (((1,), (1,)), ((), ())), preferred_element_type=jnp.float32
     )
-    local_scores = lax.psum(partial_value, ("vocab", "grp"))
+    local_scores = lax.psum(lax.psum(partial_value, "grp"), "vocab")
     scores = lax.all_gather(local_scores, "enc", axis=1, tiled=True)
     loss_sum, score_grad = softmax_grads(scores, positives)
     batch_loss = loss_sum / scores.shape[0]

time: 363 us -> 352 us (0.970)
  blocking collectives: 50 us -> 42.6 us
  waiting for transfers between devices: 248 us -> 244 us
    psum x1 -> x2, blocking collectives: 34.3 us -> 27 us  [per_device(): local_scores = lax.psum(lax.psum(partial_value, 'grp'), 'vocab')]
    reduce_scatter x1, waiting for transfers between devices: 61.7 us -> 57.8 us  [per_device(): lax.psum_scatter(jnp.dot(own_grad, pass_reps, preferred_element_type=jnp....]
  transfers between devices with their start and end apart: 5 -> 5, of which waited for: 5 -> 5; matrix products, arithmetic and copies ran while one was open for 12% -> 13% of each run, Pallas kernels for 0% -> 0%
where the time goes in v1:
time: 352 us
  waiting for transfers between devices  244 us (69%)
  blocking collectives  42.6 us (12%)
  matrix products  37.8 us (11%)
  between operations  15.6 us (4%)
  other arithmetic  12 us (3%)
    all_gather x1, waiting for transfers between devices, per_device(): lax.all_gather(head_weight, 'enc', axis=0, tiled=True)  82.1 us
    reduce_scatter x1, waiting for transfers between devices, per_device(): lax.psum_scatter(jnp.dot(own_grad, pass_reps, preferred_element_type=jnp....  57.8 us
    all_gather x1, waiting for transfers between devices, per_device(): features_all = lax.all_gather(hidden, ('vocab', 'grp'), axis=1, tiled=True)  50.6 us
    all_gather x1, waiting for transfers between devices, project(): lax.all_gather(dense_weight, 'enc', axis=0, tiled=True)  41.4 us
    psum x2, blocking collectives, per_device(): local_scores = lax.psum(lax.psum(partial_value, 'grp'), 'vocab')  27 us
    dot_general x1, matrix products, per_device(): jnp.dot(normed, lax.all_gather(head_weight, 'enc', axis=0, tiled=True), p...  21.4 us
    all_gather x1, blocking collectives, per_device(): scores = lax.all_gather(local_scores, 'enc', axis=1, tiled=True)  15.7 us
    dot_general x1, matrix products, project(): jnp.dot(in_rows, lax.all_gather(dense_weight, 'enc', axis=0, tiled=True),...  10.5 us
  transfers between devices with their start and end apart: 5, of which 5 were waited for; matrix products, arithmetic and copies ran while one was open for 13% of the time, Pallas kernels for 0%

profile of v1, /device:TPU:2, one launch (start us, length us, event | category | flops | bytes accessed | tf_op | source)
XLA Modules:
  0.0 351.9 jit_solution(11377642667303253711)
XLA Ops:
  7.2 0.0 all-gather.6.cloned.1.call-start
  7.2 0.7 all-gather.6.cloned.1.call-update
  7.9 0.0 all-gather.8.cloned.1.call-start
  7.9 0.7 all-gather.8.cloned.1.call-update
  8.6 0.0 all-gather.10.cloned.1.call-start
  8.7 0.7 all-gather.10.cloned.1.call-update
  9.4 0.0 all-gather.12.cloned.1.call-start
  9.4 0.5 all-gather.12.cloned.1.call-update
  10.0 0.0 reduce-scatter.2.cloned.1.call-start
  10.0 0.7 iota_compare_fusion.1
  10.7 0.7 iota_compare_fusion
  11.4 50.6 %all-gather.6.cloned.1.call-done = bf16[768,1024]{0,1:T(8,128)(2,1)} async-done(((bf16[768,64]{0,1:T(8,128)(2,1)}), bf16[768,1024]{0,1:T(8,128)(2,1)}) %all-gather.6.cloned.1.call-update) | async-done | bytes 1572880 | tf_op jit(solution)/shard_map/all_gather | solution.py:50
  62.0 41.4 %all-gather.8.cloned.1.call-done = bf16[1024,1024]{1,0:T(8,128)(2,1)} async-done(((bf16[64,1024]{1,0:T(8,128)(2,1)}), bf16[1024,1024]{1,0:T(8,128)(2,1)}) %all-gather.8.cloned.1.call-update) | async-done | bytes 2097168 | tf_op jit(solution)/shard_map/all_gather | solution.py:17
  103.4 10.5 %fusion.17 = (f32[768]{0:T(1024)S(1)}, f32[768,1024]{1,0:T(8,128)S(1)}) fusion(bf16[768,1024]{0,1:T(8,128)(2,1)} %all-gather.6.cloned.1.call-done, bf16[1024,1024]{1,0:T(8,128)(2,1)} %all-gather.8.cloned.1.call-done), kind=kOutput, calls=%fused_computation.41 | convolution fusion | flops 1661730048 | bytes 6818816 | tf_op jit(solution)/shard_map/dot_general | solution.py:15
  114.0 0.0 copy-start.2
  114.0 0.4 multiply_reduce_fusion
  114.5 82.1 %all-gather.10.cloned.1.call-done = bf16[1024,7936]{1,0:T(8,128)(2,1)} async-done(((bf16[64,7936]{1,0:T(8,128)(2,1)}), bf16[1024,7936]{1,0:T(8,128)(2,1)}) %all-gather.10.cloned.1.call-update) | async-done | bytes 16252944 | tf_op jit(solution)/shard_map/all_gather | solution.py:54
  196.5 0.0 copy-done.2
  196.5 21.4 %convolution_add_fusion = f32[768,7936]{1,0:T(8,128)} fusion(bf16[1024,7936]{1,0:T(8,128)(2,1)} %all-gather.10.cloned.1.call-done, f32[7936]{0:T(1024)S(1)} %copy-done.2, f32[768,1024]{1,0:T(8,128)S(1)} %get-tuple-element.8, f32[768]{0:T(1024)S(1)} %add_rsqrt_fusion, f32[768]{0:T(1024)S(1)} %broadcast_multiply_fusion), kind=kOutput, calls=%fused_computation.1 | convolution fusion | flops 12490702848 | bytes 43815936 | tf_op jit(solution)/shard_map/dot_general | solution.py:52
  217.9 9.4 %select_reduce_fusion = f32[3,7936]{1,0:T(4,128)S(1)} fusion(f32[3,256,7936]{2,1,0:T(8,128)} %bitcast.14, pred[3,256]{1,0:T(4,128)(4,1)S(1)} %iota_compare_fusion.1), kind=kLoop, calls=%fused_computation | loop fusion | flops 12165888 | bytes 24475392 | tf_op jit(solution)/shard_map/reduce_max | solution.py:29
  227.4 9.2 %all-gather.12.cloned.1.call-done = bf16[128,7936]{1,0:T(8,128)(2,1)} async-done(((bf16[8,7936]{1,0:T(8,128)(2,1)}), bf16[128,7936]{1,0:T(8,128)(2,1)}) %all-gather.12.cloned.1.call-update) | async-done | bytes 2031632 | tf_op jit(solution)/shard_map/all_gather | solution.py:58
  236.5 2.2 convolution_bitcast_fusion
  238.7 5.0 %psum.14 = f32[128,3]{0,1:T(4,128)S(1)} all-reduce(f32[128,3]{0,1:T(4,128)S(1)} %convolution_bitcast_fusion), channel_id=1, replica_groups=mesh['enc'=16,'vocab'=8,'grp'=2] {'grp'}, use_global_device_ids=true, to_apply=%region_3.4 | all-reduce | flops 384 | bytes 3072 | tf_op jit(solution)/shard_map/psum | solution.py:62
  243.7 22.0 %psum.15 = f32[128,3]{0,1:T(4,128)S(1)} all-reduce(f32[128,3]{0,1:T(4,128)S(1)} %psum.14), channel_id=1, replica_groups=mesh['enc'=16,'vocab'=8,'grp'=2] {'vocab'}, use_global_device_ids=true, to_apply=%region_4.5 | all-reduce | flops 384 | bytes 3072 | tf_op jit(solution)/shard_map/psum | solution.py:62
  265.7 15.7 %all-gather = f32[16,3,128]{2,1,0:T(4,128)S(1)} all-gather(f32[1,3,128]{2,1,0:T(4,128)S(1)} %bitcast.17), channel_id=1, replica_groups=mesh['enc'=16,'vocab'=8,'grp'=2] {'enc'}, dimensions={0}, use_global_device_ids=true | all-gather | bytes 26112 | tf_op jit(solution)/shard_map/all_gather | solution.py:63
  281.4 0.0 copy-done.1
  281.4 0.6 subtract_reduce_fusion
  282.0 2.7 fusion.14
  284.7 0.0 reduce-scatter.2.cloned.1.call-update
  285.4 0.0 copy-done
  285.4 1.0 fusion.20
  286.4 57.8 %reduce-scatter.2.cloned.1.call-done = f32[8,7936]{1,0:T(8,128)} async-done(((f32[128,7936]{1,0:T(8,128)}), f32[8,7936]{1,0:T(8,128)}) %reduce-scatter.2.cloned.1.call-update) | async-done | bytes 253968 | tf_op jit(solution)/shard_map/reduce_scatter | solution.py:67
  (7 shorter events, 0.1 us)
Async XLA Ops:
  7.2 54.9 %all-gather.6.cloned.1.call-start = ((), (), s32[]{:S(2)}) async-start(), calls=%async_computation.1 | async-start | bytes 1671168 | tf_op jit(solution)/shard_map/all_gather | solution.py:50
  7.9 95.5 %all-gather.8.cloned.1.call-start = ((), (), s32[]{:S(2)}) async-start(), calls=%async_computation.2 | async-start | bytes 2228224 | tf_op jit(solution)/shard_map/all_gather | solution.py:17
  8.6 187.9 %all-gather.10.cloned.1.call-start = ((), (), s32[]{:S(2)}) async-start(), calls=%async_computation.3 | async-start | bytes 17268736 | tf_op jit(solution)/shard_map/all_gather | solution.py:54
  9.4 227.2 %all-gather.12.cloned.1.call-start = ((), (), s32[]{:S(2)}) async-start(), calls=%async_computation.4 | async-start | bytes 2158592 | tf_op jit(solution)/shard_map/all_gather | solution.py:58
  10.0 334.3 %reduce-scatter.2.cloned.1.call-start = ((), (), s32[]{:S(2)}) async-start(), calls=%async_computation.5 | async-start | bytes 4317184 | tf_op jit(solution)/shard_map/reduce_scatter | solution.py:67
  114.0 82.6 %copy-start.2 = (f32[7936]{0:T(1024)S(1)}, f32[7936]{0:T(1024)}, u32[]{:S(2)}) copy-start(f32[7936]{0:T(1024)} %param.10) | copy-start | bytes 95236
  217.9 63.5 %copy-start.1 = (s32[128]{0:T(128)S(1)}, s32[128]{0:T(128)}, u32[]{:S(2)}) copy-start(s32[128]{0:T(128)} %param.13) | copy-start | bytes 1540
  282.0 3.3 copy-start
Sparse Core Ops, SparseCore 0:
  10.5 51.5 all-gather.5
  63.9 39.5 all-gather.7
  105.3 91.2 all-gather.9
  198.2 38.2 all-gather.11
  284.8 59.3 reduce-scatter.1
